TPU v7x, 32 devices: a whole 2x2x4 slice. The times are simulated.
32 devices in a mesh: row: 4 (over z), leaf: 8 (over y, x, core).
Axes of the slice: x: 2, y: 2, z: 4, core: 2. Of those that a mesh axis runs over, the one named last changes fastest.
Arguments:
- leaf_update: float32 [16384, 256], P(('leaf', 'row')), may hold values from -6 to 6
- rhs: float32 [3, 16384, 256], P(None, ('leaf', 'row')), may hold values from -6 to 6
- inv_top: bfloat16 [2, 16384, 8, 4, 512], P(None, 'leaf', None, 'row'), may hold values from -0.03125 to 0.03125
- inv_mid: bfloat16 [2, 16384, 4, 4, 512], P(None, 'leaf', None, 'row'), may hold values from -0.046875 to 0.046875
- inv_low: bfloat16 [2, 16384, 2, 4, 512], P(None, 'leaf', None, 'row'), may hold values from -0.0625 to 0.0625
- couple_mid: bfloat16 [2, 16384, 4, 4, 512], P(None, 'leaf', None, 'row'), may hold values from -0.046875 to 0.046875
- couple_low: bfloat16 [2, 16384, 2, 4, 512], P(None, 'leaf', None, 'row'), may hold values from -0.0625 to 0.0625
- block_map: int32 [3, 128], P(None, ('leaf', 'row')), may hold values from 0 to 127, as said below
Outputs:
- solution: float32 [3, 16384, 256], P(None, ('leaf', 'row'))
- leaf_solution: float32 [16384, 256], P(('leaf', 'row'))
Inputs may be any that keep to these rules, and one draw needn't show every extreme that they name: Device d of the group of a front holds rows d * 512 to (d + 1) * 512 - 1 of the front's separator part and the same rows of its update part, with d = p * 4 + r for group position p (leaf index modulo the group size) and row index r. block_map[k] is one to one within each parent, and a block held at row index r and group position p of a child lands on a parent block held at row index r and group position p or p + (group size of the parent) / 2. At level 0 every parent block receives one block.
All inputs are finite; a program needn't handle non-finite values.
Results may differ from a plain program's by a relative error of at most 0.012.
Values may be sent and summed in bfloat16 or wider, within the bound.
A program may use at most 256 MiB of HBM per device.

v0:
```python
import jax
import jax.numpy as jnp
from jax import lax
from jax.sharding import PartitionSpec as P

BLOCK = 128


def partner_2(block, axis, distance):
    count = lax.axis_size(axis)
    route = []
    for low in range(count):
        high = low | 1 << distance
        if high != low and high < count:
            route += [(low, high), (high, low)]
    return lax.ppermute(block, axis, route)


def turned(vector):
    half_cols = vector.shape[1] // 2
    return jnp.stack(
        [vector, jnp.concatenate([-vector[:, half_cols:], vector[:, :half_cols]], axis=1)]
    )


def forward_apply(panel_tile, vector):
    positions, width = (panel_tile.shape[2], panel_tile.shape[4])
    return lax.dot_general(
        panel_tile[:, :, :, 0, :],
        turned(vector).reshape(2, positions, width, -1),
        (((0, 2, 3), (0, 1, 2)), ((), ())),
        preferred_element_type=jnp.float32,
    )


def transposed_apply(panel_tile, vector):
    product = lax.dot_general(
        panel_tile[:, :, :, 0, :],
        turned(vector),
        (((0, 1), (0, 1)), ((), ())),
        preferred_element_type=jnp.float32,
    )
    return product.reshape(-1, vector.shape[1])


def gather_in_order(vector, order, leaf_pos):
    bit_count = len(order)
    gathered = vector[None]
    done = []
    for bit_pos in order:
        partner = partner_2(gathered, "leaf", bit_pos)
        higher = [pos for pos in done if pos > bit_pos]
        done.append(bit_pos)
        outer = 1 << len(higher)
        mine = gathered.reshape(outer, 1, -1, *vector.shape)
        theirs = partner.reshape(mine.shape)
        upper_half = leaf_pos >> bit_pos & 1 == 1
        gathered = jnp.where(
            upper_half,
            jnp.concatenate([theirs, mine], axis=1),
            jnp.concatenate([mine, theirs], axis=1),
        ).reshape(-1, *vector.shape)
    return gathered.reshape((1 << bit_count) * vector.shape[0], vector.shape[1])


def subgroup_gather(vector, bit_count, leaf_pos):
    if bit_count < 3:
        return gather_in_order(vector, list(range(bit_count))[::-1], leaf_pos)
    outer_bits = list(range(1, bit_count))
    half_cols = vector.shape[1] // 2
    first = gather_in_order(vector[:, :half_cols], outer_bits + [0], leaf_pos)
    second = gather_in_order(vector[:, half_cols:], outer_bits[::-1] + [0], leaf_pos)
    return jnp.concatenate([first, second], axis=1)


def halved_sum(total, order, leaf_pos, left):
    for bit_pos in order:
        axis = left.index(bit_pos)
        mine = leaf_pos >> bit_pos & 1
        keep = lax.dynamic_index_in_dim(total, mine, axis, keepdims=False)
        give = lax.dynamic_index_in_dim(total, 1 - mine, axis, keepdims=False)
        got = partner_2(give.astype(jnp.bfloat16), "leaf", bit_pos)
        total = keep + got.astype(jnp.float32)
        left = [pos for pos in left if pos != bit_pos]
    return total


def subgroup_sum(partial_value, bit_count, leaf_pos):
    rows = partial_value.shape[0] >> bit_count
    columns = partial_value.shape[1]
    total = partial_value.reshape((2,) * bit_count + (rows, columns))
    left = list(range(bit_count))[::-1]
    if bit_count < 3:
        return halved_sum(total, left[::-1], leaf_pos, left)
    total = halved_sum(total, [0], leaf_pos, left)
    left = left[:-1]
    half_cols = columns // 2
    first = halved_sum(total[..., :half_cols], left, leaf_pos, left)
    second = halved_sum(total[..., half_cols:], left[::-1], leaf_pos, left)
    return jnp.concatenate([first, second], axis=1)


def row_reduced(panel_tile, gathered):
    partial_value = forward_apply(panel_tile, gathered).astype(jnp.bfloat16)
    return lax.psum_scatter(partial_value, "row", scatter_dimension=0, tiled=True).astype(
        jnp.float32
    )


def row_folded(panel_tile, vector_half):
    return transposed_apply(panel_tile, lax.all_gather(vector_half, "row", axis=0, tiled=True))


def slot_ids(position, row_pos, row_size, blocks_dev, sep_blocks, has_update):
    own_slots = (position * row_size + row_pos) * blocks_dev + jnp.arange(
        blocks_dev, dtype=jnp.int32
    )
    if has_update:
        return jnp.concatenate([own_slots, own_slots + sep_blocks])
    return own_slots


def extend_add(child_rows, targets, rhs_part, bit_count, has_update, leaf_pos, row_pos, row_size):
    bit_pos = bit_count - 1
    partner_targets = partner_2(targets, "leaf", bit_pos)
    partner_rows = partner_2(child_rows.astype(jnp.bfloat16), "leaf", bit_pos).astype(jnp.float32)
    blocks_dev = targets.shape[0]
    group_size = 1 << bit_count
    position = leaf_pos & group_size - 1
    sep_blocks = group_size * row_size * blocks_dev
    slot_list = slot_ids(position, row_pos, row_size, blocks_dev, sep_blocks, has_update)
    candidates = jnp.concatenate([targets, partner_targets])
    columns = child_rows.shape[1]
    block_pool = jnp.concatenate([child_rows, partner_rows], axis=0).reshape(2 * blocks_dev, -1)
    selector = (slot_list[:, None] == candidates[None, :]).astype(jnp.float32)
    placed = jnp.dot(
        selector, block_pool, precision=lax.Precision.HIGHEST, preferred_element_type=jnp.float32
    ).reshape(-1, columns)
    slice_rows = rhs_part.shape[0]
    return (placed[:slice_rows] + rhs_part, placed[slice_rows:])


def extend_down(front_parts, targets, bit_count, leaf_pos, row_pos, row_size):
    bit_pos = bit_count - 1
    partner_parts = [
        partner_2(part.astype(jnp.bfloat16), "leaf", bit_pos).astype(jnp.float32)
        for part in front_parts
    ]
    blocks_dev = targets.shape[0]
    has_update = len(front_parts) > 1
    group_size = 1 << bit_count
    position = leaf_pos & group_size - 1
    sep_blocks = group_size * row_size * blocks_dev
    own_slots = slot_ids(position, row_pos, row_size, blocks_dev, sep_blocks, has_update)
    partner_slots = slot_ids(
        position ^ group_size // 2, row_pos, row_size, blocks_dev, sep_blocks, has_update
    )
    columns = front_parts[0].shape[1]
    block_pool = jnp.concatenate([*front_parts, *partner_parts], axis=0).reshape(
        -1, BLOCK * columns
    )
    selector = (targets[:, None] == jnp.concatenate([own_slots, partner_slots])[None, :]).astype(
        jnp.float32
    )
    return jnp.dot(
        selector, block_pool, precision=lax.Precision.HIGHEST, preferred_element_type=jnp.float32
    ).reshape(-1, columns)


def shards(leaf_update, rhs, inv_top, inv_mid, inv_low, couple_mid, couple_low, block_map):
    leaf_pos = lax.axis_index("leaf")
    row_pos = lax.axis_index("row")
    row_size = lax.axis_size("row")
    leaf_bits = lax.axis_size("leaf").bit_length() - 1
    inverses = (inv_top, inv_mid, inv_low)
    couplings = (None, couple_mid, couple_low)
    children = leaf_update
    saved_y = [None, None, None]
    for level_index in (2, 1):
        bit_count = leaf_bits - level_index
        sep_part, update_part = extend_add(
            children,
            block_map[level_index],
            rhs[level_index],
            bit_count,
            True,
            leaf_pos,
            row_pos,
            row_size,
        )
        gathered = subgroup_gather(sep_part.astype(jnp.bfloat16), bit_count, leaf_pos)
        solved = row_reduced(inverses[level_index], gathered)
        saved_y[level_index] = solved
        gathered_y = subgroup_gather(solved.astype(jnp.bfloat16), bit_count, leaf_pos)
        children = update_part - row_reduced(couplings[level_index], gathered_y)
    sep_top, unused_rows = extend_add(
        children, block_map[0], rhs[0], leaf_bits, False, leaf_pos, row_pos, row_size
    )
    gathered = subgroup_gather(sep_top.astype(jnp.bfloat16), leaf_bits, leaf_pos)
    y_top = row_reduced(inv_top, gathered)
    partial_value = row_folded(inv_top, y_top.astype(jnp.bfloat16))
    x_top = subgroup_sum(partial_value, leaf_bits, leaf_pos)
    solutions = [x_top]
    front_parts = [x_top]
    for level_index in (1, 2):
        bit_count = leaf_bits - level_index
        x_update = extend_down(
            front_parts, block_map[level_index - 1], bit_count + 1, leaf_pos, row_pos, row_size
        )
        coupled = subgroup_sum(
            row_folded(couplings[level_index], x_update.astype(jnp.bfloat16)), bit_count, leaf_pos
        )
        reduced = saved_y[level_index] - coupled
        x_sep = subgroup_sum(
            row_folded(inverses[level_index], reduced.astype(jnp.bfloat16)), bit_count, leaf_pos
        )
        solutions.append(x_sep)
        front_parts = [x_sep, x_update]
    leaf_solution = extend_down(
        front_parts, block_map[2], leaf_bits - 2, leaf_pos, row_pos, row_size
    )
    return (jnp.stack(solutions), leaf_solution)


def solution(mesh):
    return jax.shard_map(
        shards,
        mesh=mesh,
        in_specs=(
            P(("leaf", "row"), None),
            P(None, ("leaf", "row"), None),
            P(None, "leaf", None, "row", None),
            P(None, "leaf", None, "row", None),
            P(None, "leaf", None, "row", None),
            P(None, "leaf", None, "row", None),
            P(None, "leaf", None, "row", None),
            P(None, ("leaf", "row")),
        ),
        out_specs=(P(None, ("leaf", "row"), None), P(("leaf", "row"), None)),
        check_vma=False,
    )
```

profile of v0, /device:TPU:0, one launch (start us, length us, event | category | flops | bytes accessed | tf_op | source)
XLA Modules:
  0.0 577.8 jit_solution(7847423660793290802)
XLA Ops:
  15.6 6.7 %fusion.67 = bf16[2048,256]{0,1:T(8,128)(2,1)} fusion(bf16[2,2048,2,512]{3,2,1,0:T(2,128)(2,1)} %bitcast.316, bf16[1,2,512,256]{2,3,1,0:T(8,128)(2,1)S(1)} %copy.43, bf16[1,2,512,256]{2,3,1,0:T(8,128)(2,1)S(1)} %fusion.173), kind=kOutput, calls=%fused_computation.39 | convolution fusion | flops 2148532224 | bytes 10485760 | tf_op jit(solution)/shard_map/dot_general | solution.py:28
  22.4 30.0 %reduce-scatter.6.cloned.1.call-done = bf16[512,256]{0,1:T(8,128)(2,1)} async-done(((bf16[2048,256]{0,1:T(8,128)(2,1)}), bf16[512,256]{0,1:T(8,128)(2,1)}) %reduce-scatter.6.cloned.1.call-update) | async-done | bytes 262160 | tf_op jit(solution)/shard_map/reduce_scatter | solution.py:105
  57.0 6.7 %fusion.70 = bf16[2048,256]{0,1:T(8,128)(2,1)} fusion(bf16[2,2048,2,512]{3,2,1,0:T(2,128)(2,1)} %bitcast.314, bf16[1,2,512,256]{2,3,1,0:T(8,128)(2,1)S(1)} %copy.46, bf16[1,2,512,256]{2,3,1,0:T(8,128)(2,1)S(1)} %fusion.172), kind=kOutput, calls=%fused_computation.40 | convolution fusion | flops 2148532224 | bytes 10485760 | tf_op jit(solution)/shard_map/dot_general | solution.py:28
  66.1 23.6 %reduce-scatter.8.cloned.1.call-done = bf16[512,256]{0,1:T(8,128)(2,1)} async-done(((bf16[2048,256]{0,1:T(8,128)(2,1)}), bf16[512,256]{0,1:T(8,128)(2,1)}) %reduce-scatter.8.cloned.1.call-update) | async-done | bytes 262160 | tf_op jit(solution)/shard_map/reduce_scatter | solution.py:105
  92.6 5.8 %collective-permute-done.6 = bf16[512,256]{0,1:T(8,128)(2,1)S(1)} collective-permute-done((bf16[512,256]{0,1:T(8,128)(2,1)S(1)}, bf16[512,256]{0,1:T(8,128)(2,1)S(1)}, u32[]{:S(2)}, u32[]{:S(2)}) %collective-permute-start.6) | collective-permute-done | bytes 262176 | tf_op jit(solution)/shard_map/ppermute | solution.py:16
  112.8 12.4 %fusion.61 = bf16[2048,256]{0,1:T(8,128)(2,1)} fusion(bf16[2,2048,4,512]{3,2,1,0:T(4,128)(2,1)} %bitcast.312, bf16[1,4,512,256]{2,3,1,0:T(8,128)(2,1)} %copy.54, bf16[1,4,512,256]{2,3,1,0:T(8,128)(2,1)S(1)} %bitcast.293), kind=kOutput, calls=%fused_computation.37 | convolution fusion | flops 4296540160 | bytes 19922944 | tf_op jit(solution)/shard_map/dot_general | solution.py:28
  125.7 26.2 %reduce-scatter.10.cloned.1.call-done = bf16[512,256]{0,1:T(8,128)(2,1)} async-done(((bf16[2048,256]{0,1:T(8,128)(2,1)}), bf16[512,256]{0,1:T(8,128)(2,1)}) %reduce-scatter.10.cloned.1.call-update) | async-done | bytes 262160 | tf_op jit(solution)/shard_map/reduce_scatter | solution.py:105
  153.4 6.4 %collective-permute-done.9 = bf16[1,512,256]{1,2,0:T(8,128)(2,1)S(1)} collective-permute-done((bf16[1,512,256]{1,2,0:T(8,128)(2,1)}, bf16[1,512,256]{1,2,0:T(8,128)(2,1)S(1)}, u32[]{:S(2)}, u32[]{:S(2)}) %collective-permute-start.9) | collective-permute-done | bytes 262176 | tf_op jit(solution)/shard_map/ppermute | solution.py:16
  165.1 12.4 %fusion.64 = bf16[2048,256]{0,1:T(8,128)(2,1)} fusion(bf16[2,2048,4,512]{3,2,1,0:T(4,128)(2,1)} %bitcast.310, bf16[1,4,512,256]{2,3,1,0:T(8,128)(2,1)} %copy.59, bf16[1,4,512,256]{2,3,1,0:T(8,128)(2,1)S(1)} %bitcast.261), kind=kOutput, calls=%fused_computation.38 | convolution fusion | flops 4296540160 | bytes 19922944 | tf_op jit(solution)/shard_map/dot_general | solution.py:28
  178.2 25.6 %reduce-scatter.12.cloned.1.call-done = bf16[512,256]{0,1:T(8,128)(2,1)} async-done(((bf16[2048,256]{0,1:T(8,128)(2,1)}), bf16[512,256]{0,1:T(8,128)(2,1)}) %reduce-scatter.12.cloned.1.call-update) | async-done | bytes 262160 | tf_op jit(solution)/shard_map/reduce_scatter | solution.py:105
  233.4 19.6 %fusion.73 = bf16[2048,256]{0,1:T(8,128)(2,1)} fusion(bf16[2,2048,8,512]{3,2,1,0:T(8,128)(2,1)} %bitcast.308, bf16[1,8,512,128]{2,3,1,0:T(8,128)(2,1)S(1)} %bitcast.287, bf16[1,8,512,128]{2,3,1,0:T(8,128)(2,1)S(1)} %neg.39, bf16[1,8,512,128]{2,3,1,0:T(8,128)(2,1)S(1)} %bitcast.263), kind=kOutput, calls=%fused_computation.41 | convolution fusion | flops 8607236096 | bytes 37748736 | tf_op jit(solution)/shard_map/dot_general | solution.py:28
  253.0 25.0 %reduce-scatter.14.cloned.1.call-done = bf16[512,256]{0,1:T(8,128)(2,1)} async-done(((bf16[2048,256]{0,1:T(8,128)(2,1)}), bf16[512,256]{0,1:T(8,128)(2,1)}) %reduce-scatter.14.cloned.1.call-update) | async-done | bytes 262160 | tf_op jit(solution)/shard_map/reduce_scatter | solution.py:105
  278.3 27.7 %all-gather.6.cloned.1.call-done = bf16[2048,256]{0,1:T(8,128)(2,1)} async-done(((bf16[512,256]{0,1:T(8,128)(2,1)}), bf16[2048,256]{0,1:T(8,128)(2,1)}) %all-gather.6.cloned.1.call-update) | async-done | bytes 1048592 | tf_op jit(solution)/shard_map/all_gather | solution.py:111
  307.5 23.9 %fusion = f32[256,8,512,1]{2,0,3,1:T(8,128)} fusion(bf16[2,2048,8,512]{3,2,1,0:T(8,128)(2,1)} %bitcast.309, bf16[1,2048,256]{1,2,0:T(8,128)(2,1)S(1)} %maximum_bitcast_fusion.14, bf16[1,2048,256]{1,2,0:T(8,128)(2,1)S(1)} %bitcast.288), kind=kOutput, calls=%fused_computation | convolution fusion | flops 8594128896 | bytes 39845888 | tf_op jit(solution)/shard_map/dot_general | solution.py:37
  362.7 26.3 %all-gather.8.cloned.1.call-done = bf16[2048,256]{0,1:T(8,128)(2,1)} async-done(((bf16[512,256]{0,1:T(8,128)(2,1)}), bf16[2048,256]{0,1:T(8,128)(2,1)}) %all-gather.8.cloned.1.call-update) | async-done | bytes 1048592 | tf_op jit(solution)/shard_map/all_gather | solution.py:111
  390.6 8.2 %fusion.6 = f32[256,4,512,1]{2,0,3,1:T(8,128)S(1)} fusion(bf16[2,2048,4,512]{3,2,1,0:T(4,128)(2,1)} %bitcast.311, bf16[1,2048,256]{1,2,0:T(8,128)(2,1)S(1)} %maximum_bitcast_fusion.15, bf16[1,2048,256]{1,2,0:T(8,128)(2,1)S(1)} %bitcast.290), kind=kOutput, calls=%fused_computation.6 | convolution fusion | flops 4299161600 | bytes 20971520 | tf_op jit(solution)/shard_map/dot_general | solution.py:37
  407.6 6.8 %collective-permute-done.25 = bf16[512,256]{0,1:T(8,128)(2,1)S(1)} collective-permute-done((bf16[512,256]{0,1:T(8,128)(2,1)S(1)}, bf16[512,256]{0,1:T(8,128)(2,1)S(1)}, u32[]{:S(2)}, u32[]{:S(2)}) %collective-permute-start.25) | collective-permute-done | bytes 262176 | tf_op jit(solution)/shard_map/ppermute | solution.py:16
  415.3 27.5 %all-gather.10.cloned.1.call-done = bf16[2048,256]{0,1:T(8,128)(2,1)} async-done(((bf16[512,256]{0,1:T(8,128)(2,1)}), bf16[2048,256]{0,1:T(8,128)(2,1)}) %all-gather.10.cloned.1.call-update) | async-done | bytes 1048592 | tf_op jit(solution)/shard_map/all_gather | solution.py:111
  444.3 8.2 %fusion.4 = f32[256,4,512,1]{2,0,3,1:T(8,128)S(1)} fusion(bf16[2,2048,4,512]{3,2,1,0:T(4,128)(2,1)} %bitcast.313, bf16[1,2048,256]{1,2,0:T(8,128)(2,1)S(1)} %maximum_bitcast_fusion.16, bf16[1,2048,256]{1,2,0:T(8,128)(2,1)S(1)} %bitcast.289), kind=kOutput, calls=%fused_computation.4 | convolution fusion | flops 4299161600 | bytes 20971520 | tf_op jit(solution)/shard_map/dot_general | solution.py:37
  462.0 7.1 %collective-permute-done.27 = bf16[512,256]{0,1:T(8,128)(2,1)S(1)} collective-permute-done((bf16[512,256]{0,1:T(8,128)(2,1)S(1)}, bf16[512,256]{0,1:T(8,128)(2,1)S(1)}, u32[]{:S(2)}, u32[]{:S(2)}) %collective-permute-start.27) | collective-permute-done | bytes 262176 | tf_op jit(solution)/shard_map/ppermute | solution.py:16
  485.6 27.2 %all-gather.12.cloned.1.call-done = bf16[2048,256]{0,1:T(8,128)(2,1)} async-done(((bf16[512,256]{0,1:T(8,128)(2,1)}), bf16[2048,256]{0,1:T(8,128)(2,1)}) %all-gather.12.cloned.1.call-update) | async-done | bytes 1048592 | tf_op jit(solution)/shard_map/all_gather | solution.py:111
  514.4 5.7 fusion.94
  522.6 27.5 %all-gather.14.cloned.1.call-done = bf16[2048,256]{0,1:T(8,128)(2,1)} async-done(((bf16[512,256]{0,1:T(8,128)(2,1)}), bf16[2048,256]{0,1:T(8,128)(2,1)}) %all-gather.14.cloned.1.call-update) | async-done | bytes 1048592 | tf_op jit(solution)/shard_map/all_gather | solution.py:111
  551.7 5.7 fusion.97
  (286 shorter events, 159.7 us)
Async XLA Ops:
  7.2 45.3 %reduce-scatter.6.cloned.1.call-start = ((), (), s32[]{:S(2)}) async-start(), calls=%async_computation.5 | async-start | bytes 1310720 | tf_op jit(solution)/shard_map/reduce_scatter | solution.py:105
  22.4 67.3 %reduce-scatter.8.cloned.1.call-start = ((), (), s32[]{:S(2)}) async-start(), calls=%async_computation.6 | async-start | bytes 1310720 | tf_op jit(solution)/shard_map/reduce_scatter | solution.py:105
  63.7 88.2 %reduce-scatter.10.cloned.1.call-start = ((), (), s32[]{:S(2)}) async-start(), calls=%async_computation.7 | async-start | bytes 1310720 | tf_op jit(solution)/shard_map/reduce_scatter | solution.py:105
  64.0 28.6 %collective-permute-start.1 = (s32[4]{0:T(128)S(1)}, s32[4]{0:T(128)S(1)}, u32[]{:S(2)}, u32[]{:S(2)}) collective-permute-start(s32[4]{0:T(128)S(1)} %get-tuple-element.46), channel_id=1, source_target_pairs={{0,2},{2,0},{1,3},{3,1},{4,6},{6,4},{5,7},{7,5},{8,10},{10,8},{9,1... | collective-permute-start | bytes 56 | tf_op jit(solution)/shard_map/ppermute | solution.py:16
  90.7 7.7 %collective-permute-start.6 = (bf16[512,256]{0,1:T(8,128)(2,1)S(1)}, bf16[512,256]{0,1:T(8,128)(2,1)S(1)}, u32[]{:S(2)}, u32[]{:S(2)}) collective-permute-start(bf16[512,256]{0,1:T(8,128)(2,1)S(1)} %get-tuple-element.12), channel_id=1, source_target_pairs={{0,2},{2,0},{1,3},{3,1},{4,6},{6,4},{5,7},{7,5},{8,10},{10,8},{9,1... | collective-permute-start | bytes 786440 | tf_op jit(solution)/shard_map/ppermute | solution.py:16
  100.6 6.9 %collective-permute-start.7 = (bf16[1,512,256]{1,2,0:T(8,128)(2,1)S(1)}, bf16[1,512,256]{1,2,0:T(8,128)(2,1)S(1)}, u32[]{:S(2)}, u32[]{:S(2)}) collective-permute-start(bf16[1,512,256]{1,2,0:T(8,128)(2,1)S(1)} %add_convert_fusion), channel_id=1, source_target_pairs={{0,2},{2,0},{1,3},{3,1},{4,6},{6,4},{5,7},{7,5},{8,10},{10,8},{9,1... | collective-permute-start | bytes 786440 | tf_op jit(solution)/shard_map/ppermute | solution.py:16
  125.3 78.6 %reduce-scatter.12.cloned.1.call-start = ((), (), s32[]{:S(2)}) async-start(), calls=%async_computation.8 | async-start | bytes 1310720 | tf_op jit(solution)/shard_map/reduce_scatter | solution.py:105
  151.9 7.9 %collective-permute-start.9 = (bf16[1,512,256]{1,2,0:T(8,128)(2,1)}, bf16[1,512,256]{1,2,0:T(8,128)(2,1)S(1)}, u32[]{:S(2)}, u32[]{:S(2)}) collective-permute-start(bf16[1,512,256]{1,2,0:T(8,128)(2,1)} %bitcast.277), channel_id=1, source_target_pairs={{0,2},{2,0},{1,3},{3,1},{4,6},{6,4},{5,7},{7,5},{8,10},{10,8},{9,1... | collective-permute-start | bytes 786440 | tf_op jit(solution)/shard_map/ppermute | solution.py:16
  177.6 100.4 %reduce-scatter.14.cloned.1.call-start = ((), (), s32[]{:S(2)}) async-start(), calls=%async_computation.9 | async-start | bytes 1310720 | tf_op jit(solution)/shard_map/reduce_scatter | solution.py:105
  204.9 7.9 %collective-permute-start.11 = (bf16[512,256]{0,1:T(8,128)(2,1)S(1)}, bf16[512,256]{0,1:T(8,128)(2,1)S(1)}, u32[]{:S(2)}, u32[]{:S(2)}) collective-permute-start(bf16[512,256]{0,1:T(8,128)(2,1)S(1)} %get-tuple-element.10), channel_id=1, source_target_pairs={{0,4},{4,0},{1,5},{5,1},{2,6},{6,2},{3,7},{7,3},{8,12},{12,8},{9,1... | collective-permute-start | bytes 786440 | tf_op jit(solution)/shard_map/ppermute | solution.py:16
  220.8 7.0 %collective-permute-start.16 = (bf16[2,512,128]{2,1,0:T(8,128)(2,1)S(1)}, bf16[2,512,128]{2,1,0:T(8,128)(2,1)S(1)}, u32[]{:S(2)}, u32[]{:S(2)}) collective-permute-start(bf16[2,512,128]{2,1,0:T(8,128)(2,1)S(1)} %maximum_select_fusion.13), channel_id=1, source_target_pairs={{0,2},{2,0},{1,3},{3,1},{4,6},{6,4},{5,7},{7,5},{8,10},{10,8},{9,1... | collective-permute-start | bytes 786440 | tf_op jit(solution)/shard_map/ppermute | solution.py:16
  223.6 6.4 %collective-permute-start.13 = (bf16[2,512,128]{2,1,0:T(8,128)(2,1)S(1)}, bf16[2,512,128]{2,1,0:T(8,128)(2,1)S(1)}, u32[]{:S(2)}, u32[]{:S(2)}) collective-permute-start(bf16[2,512,128]{2,1,0:T(8,128)(2,1)S(1)} %maximum_select_fusion.11), channel_id=1, source_target_pairs={{0,4},{4,0},{1,5},{5,1},{2,6},{6,2},{3,7},{7,3},{8,12},{12,8},{9,1... | collective-permute-start | bytes 786440 | tf_op jit(solution)/shard_map/ppermute | solution.py:16
  253.0 53.0 %all-gather.6.cloned.1.call-start = ((), (), s32[]{:S(2)}) async-start(), calls=%async_computation.10 | async-start | bytes 1310720 | tf_op jit(solution)/shard_map/all_gather | solution.py:111
  278.1 111.0 %all-gather.8.cloned.1.call-start = ((), (), s32[]{:S(2)}) async-start(), calls=%async_computation.11 | async-start | bytes 1310720 | tf_op jit(solution)/shard_map/all_gather | solution.py:111
  338.0 8.4 %collective-permute-start.21 = (bf16[2,512,128]{1,2,0:T(8,128)(2,1)S(1)}, bf16[2,512,128]{1,2,0:T(8,128)(2,1)S(1)}, u32[]{:S(2)}, u32[]{:S(2)}) collective-permute-start(bf16[2,512,128]{1,2,0:T(8,128)(2,1)S(1)} %fusion.117), channel_id=1, source_target_pairs={{0,2},{2,0},{1,3},{3,1},{4,6},{6,4},{5,7},{7,5},{8,10},{10,8},{9,1... | collective-permute-start | bytes 786440 | tf_op jit(solution)/shard_map/ppermute | solution.py:16
  339.6 8.5 %collective-permute-start.19 = (bf16[2,512,128]{1,2,0:T(8,128)(2,1)S(1)}, bf16[2,512,128]{1,2,0:T(8,128)(2,1)S(1)}, u32[]{:S(2)}, u32[]{:S(2)}) collective-permute-start(bf16[2,512,128]{1,2,0:T(8,128)(2,1)S(1)} %fusion.116), channel_id=1, source_target_pairs={{0,4},{4,0},{1,5},{5,1},{2,6},{6,2},{3,7},{7,3},{8,12},{12,8},{9,1... | collective-permute-start | bytes 786440 | tf_op jit(solution)/shard_map/ppermute | solution.py:16
  353.3 6.4 %collective-permute-start.23 = (bf16[512,256]{0,1:T(8,128)(2,1)S(1)}, bf16[512,256]{0,1:T(8,128)(2,1)S(1)}, u32[]{:S(2)}, u32[]{:S(2)}) collective-permute-start(bf16[512,256]{0,1:T(8,128)(2,1)S(1)} %fusion.114), channel_id=1, source_target_pairs={{0,4},{4,0},{1,5},{5,1},{2,6},{6,2},{3,7},{7,3},{8,12},{12,8},{9,1... | collective-permute-start | bytes 786440 | tf_op jit(solution)/shard_map/ppermute | solution.py:16
  362.4 80.3 %all-gather.10.cloned.1.call-start = ((), (), s32[]{:S(2)}) async-start(), calls=%async_computation.12 | async-start | bytes 1310720 | tf_op jit(solution)/shard_map/all_gather | solution.py:111
  406.1 8.3 %collective-permute-start.25 = (bf16[512,256]{0,1:T(8,128)(2,1)S(1)}, bf16[512,256]{0,1:T(8,128)(2,1)S(1)}, u32[]{:S(2)}, u32[]{:S(2)}) collective-permute-start(bf16[512,256]{0,1:T(8,128)(2,1)S(1)} %fusion.118), channel_id=1, source_target_pairs={{0,2},{2,0},{1,3},{3,1},{4,6},{6,4},{5,7},{7,5},{8,10},{10,8},{9,1... | collective-permute-start | bytes 786440 | tf_op jit(solution)/shard_map/ppermute | solution.py:16
  415.2 97.6 %all-gather.12.cloned.1.call-start = ((), (), s32[]{:S(2)}) async-start(), calls=%async_computation.13 | async-start | bytes 1310720 | tf_op jit(solution)/shard_map/all_gather | solution.py:111
  459.8 9.2 %collective-permute-start.27 = (bf16[512,256]{0,1:T(8,128)(2,1)S(1)}, bf16[512,256]{0,1:T(8,128)(2,1)S(1)}, u32[]{:S(2)}, u32[]{:S(2)}) collective-permute-start(bf16[512,256]{0,1:T(8,128)(2,1)S(1)} %fusion.119), channel_id=1, source_target_pairs={{0,2},{2,0},{1,3},{3,1},{4,6},{6,4},{5,7},{7,5},{8,10},{10,8},{9,1... | collective-permute-start | bytes 786440 | tf_op jit(solution)/shard_map/ppermute | solution.py:16
  461.3 13.3 %collective-permute-start.29 = (bf16[512,256]{0,1:T(8,128)(2,1)S(1)}, bf16[512,256]{0,1:T(8,128)(2,1)S(1)}, u32[]{:S(2)}, u32[]{:S(2)}) collective-permute-start(bf16[512,256]{0,1:T(8,128)(2,1)S(1)} %copy-done.7), channel_id=1, source_target_pairs={{0,2},{2,0},{1,3},{3,1},{4,6},{6,4},{5,7},{7,5},{8,10},{10,8},{9,1... | collective-permute-start | bytes 786440 | tf_op jit(solution)/shard_map/ppermute | solution.py:16
  469.1 10.2 %collective-permute-start.28 = (bf16[512,256]{0,1:T(8,128)(2,1)S(1)}, bf16[512,256]{0,1:T(8,128)(2,1)S(1)}, u32[]{:S(2)}, u32[]{:S(2)}) collective-permute-start(bf16[512,256]{0,1:T(8,128)(2,1)S(1)} %get-tuple-element.8), channel_id=1, source_target_pairs={{0,2},{2,0},{1,3},{3,1},{4,6},{6,4},{5,7},{7,5},{8,10},{10,8},{9,1... | collective-permute-start | bytes 786440 | tf_op jit(solution)/shard_map/ppermute | solution.py:16
  485.3 64.8 %all-gather.14.cloned.1.call-start = ((), (), s32[]{:S(2)}) async-start(), calls=%async_computation.14 | async-start | bytes 1310720 | tf_op jit(solution)/shard_map/all_gather | solution.py:111
  (41 other events, 148.2 us)
Sparse Core Ops, SparseCore 0:
  22.5 29.8 reduce-scatter.5
  63.8 25.7 reduce-scatter.7
  125.4 26.4 reduce-scatter.9
  177.7 26.0 reduce-scatter.11
  253.1 24.8 reduce-scatter.13
  279.5 26.4 all-gather.5
  362.6 26.4 all-gather.7
  415.3 27.3 all-gather.9
  485.4 27.3 all-gather.11
  522.7 27.3 all-gather.13
where the time goes:
time: 585 us; the launch traced here: 578 us
  waiting for transfers between devices  348 us (59%)
  matrix products  114 us (19%)
  local copies, waits for them, and re-layouts  40.2 us (7%)
  other arithmetic  31.2 us (5%)
  starting transfers between devices  29.3 us (5%)
  between operations  15.8 us (3%)
    all_gather x5, waiting for transfers between devices, row_folded(): lax.all_gather(vector_half, 'row', axis=0, tiled=True)  136 us
    reduce_scatter x5, waiting for transfers between devices, row_reduced(): lax.psum_scatter(partial_value, 'row', scatter_dimension=0, tiled=True)  130 us
    ppermute x34, waiting for transfers between devices, partner_2(): return lax.ppermute(block, axis, route)  80.7 us
    dot_general x5, matrix products, forward_apply(): lax.dot_general(panel_tile[:, :, :, 0, :], turned(vector).reshape(2, posi...  57.9 us
    dot_general x5, matrix products, transposed_apply(): lax.dot_general(panel_tile[:, :, :, 0, :], turned(vector), (((0, 1), (0,...  51.7 us
    ppermute x34, starting transfers between devices, partner_2(): return lax.ppermute(block, axis, route)  27.6 us
  transfers between devices with their start and end apart: 44, of which 34 were waited for; matrix products, arithmetic and copies ran while one was open for 4% of the time, Pallas kernels for 0%

commit v1 on v0

--- a/solution.py
+++ b/solution.py
@@ -4,6 +4,24 @@
 from jax.sharding import PartitionSpec as P
 
 BLOCK = 128
+
+
+def collect(shard, axis, dim):
+    ways, here, lap = (lax.axis_size(axis), lax.axis_index(axis), shard.shape[dim])
+    shape = [n * ways if d == dim else n for d, n in enumerate(shard.shape)]
+    full = lax.dynamic_update_slice_in_dim(
+        jnp.zeros(shape, shard.dtype), shard, here * lap, axis=dim
+    )
+    going_up = going_down = shard
+    for far in range(1, ways // 2 + 1):
+        going_up = lax.ppermute(going_up, axis, [(d, (d + 1) % ways) for d in range(ways)])
+        full = lax.dynamic_update_slice_in_dim(full, going_up, (here - far) % ways * lap, axis=dim)
+        if 2 * far < ways:
+            going_down = lax.ppermute(going_down, axis, [(d, (d - 1) % ways) for d in range(ways)])
+            full = lax.dynamic_update_slice_in_dim(
+                full, going_down, (here + far) % ways * lap, axis=dim
+            )
+    return full
 
 
 def partner_2(block, axis, distance):
@@ -108,7 +126,7 @@
 
 
 def row_folded(panel_tile, vector_half):
-    return transposed_apply(panel_tile, lax.all_gather(vector_half, "row", axis=0, tiled=True))
+    return transposed_apply(panel_tile, collect(vector_half, "row", 0))
 
 
 def slot_ids(position, row_pos, row_size, blocks_dev, sep_blocks, has_update):

time: 585 us -> 545 us (0.932)
  waiting for transfers between devices: 348 us -> 291 us
  starting transfers between devices: 29.3 us -> 47.9 us
  local copies, waits for them, and re-layouts: 40.2 us -> 52.9 us
  other arithmetic: 31.2 us -> 19.4 us
    all_gather x5 -> x0, waiting for transfers between devices: 136 us -> none  [row_folded(): lax.all_gather(vector_half, 'row', axis=0, tiled=True)]
    ppermute x0 -> x15, waiting for transfers between devices: none -> 81.4 us  [the longest x10 71.8 us: collect(): lax.ppermute(going_up, axis, [(d, (d + 1) % ways) for d in range(ways)])]
    ppermute x0 -> x15, starting transfers between devices: none -> 19.9 us  [the longest x5 19.1 us: collect(): lax.ppermute(going_down, axis, [(d, (d - 1) % ways) for d in range(ways)])]
    neg x10, other arithmetic: 7.37 us -> 0.94 us  [turned(): -vector[:, half_cols:]]
  transfers between devices with their start and end apart: 44 -> 54, of which waited for: 34 -> 43; matrix products, arithmetic and copies ran while one was open for 4% -> 6% of each run, Pallas kernels for 0% -> 0%
where the time goes in v1:
time: 545 us; the launch traced here: 538 us
  waiting for transfers between devices  291 us (53%)
  matrix products  111 us (20%)
  local copies, waits for them, and re-layouts  52.9 us (10%)
  starting transfers between devices  47.9 us (9%)
  other arithmetic  19.4 us (4%)
  between operations  15.7 us (3%)
    reduce_scatter x5, waiting for transfers between devices, row_reduced(): lax.psum_scatter(partial_value, 'row', scatter_dimension=0, tiled=True)  131 us
    ppermute x34, waiting for transfers between devices, partner_2(): return lax.ppermute(block, axis, route)  79.2 us
    ppermute x10, waiting for transfers between devices, collect(): lax.ppermute(going_up, axis, [(d, (d + 1) % ways) for d in range(ways)])  71.8 us
    dot_general x5, matrix products, forward_apply(): lax.dot_general(panel_tile[:, :, :, 0, :], turned(vector).reshape(2, posi...  57.9 us
    dot_general x5, matrix products, transposed_apply(): lax.dot_general(panel_tile[:, :, :, 0, :], turned(vector), (((0, 1), (0,...  48.5 us
    ppermute x34, starting transfers between devices, partner_2(): return lax.ppermute(block, axis, route)  27.2 us
    ppermute x5, starting transfers between devices, collect(): lax.ppermute(going_down, axis, [(d, (d - 1) % ways) for d in range(ways)])  19.1 us
  transfers between devices with their start and end apart: 54, of which 43 were waited for; matrix products, arithmetic and copies ran while one was open for 6% of the time, Pallas kernels for 0%

profile of v1, /device:TPU:0, one launch (start us, length us, event | category | flops | bytes accessed | tf_op | source)
XLA Modules:
  0.0 537.7 jit_solution(9571968614454887647)
XLA Ops:
  15.6 6.7 %fusion.67 = bf16[2048,256]{0,1:T(8,128)(2,1)} fusion(bf16[2,2048,2,512]{3,2,1,0:T(2,128)(2,1)} %bitcast.320, bf16[1,2,512,256]{2,3,1,0:T(8,128)(2,1)S(1)} %copy.39, bf16[1,2,512,256]{2,3,1,0:T(8,128)(2,1)S(1)} %fusion.175), kind=kOutput, calls=%fused_computation.39 | convolution fusion | flops 2148532224 | bytes 10485760 | tf_op jit(solution)/shard_map/dot_general | solution.py:46
  22.4 30.0 %reduce-scatter.6.cloned.1.call-done = bf16[512,256]{0,1:T(8,128)(2,1)} async-done(((bf16[2048,256]{0,1:T(8,128)(2,1)}), bf16[512,256]{0,1:T(8,128)(2,1)}) %reduce-scatter.6.cloned.1.call-update) | async-done | bytes 262160 | tf_op jit(solution)/shard_map/reduce_scatter | solution.py:123
  57.0 6.7 %fusion.70 = bf16[2048,256]{0,1:T(8,128)(2,1)} fusion(bf16[2,2048,2,512]{3,2,1,0:T(2,128)(2,1)} %bitcast.318, bf16[1,2,512,256]{2,3,1,0:T(8,128)(2,1)S(1)} %copy.42, bf16[1,2,512,256]{2,3,1,0:T(8,128)(2,1)S(1)} %fusion.174), kind=kOutput, calls=%fused_computation.40 | convolution fusion | flops 2148532224 | bytes 10485760 | tf_op jit(solution)/shard_map/dot_general | solution.py:46
  66.1 23.6 %reduce-scatter.8.cloned.1.call-done = bf16[512,256]{0,1:T(8,128)(2,1)} async-done(((bf16[2048,256]{0,1:T(8,128)(2,1)}), bf16[512,256]{0,1:T(8,128)(2,1)}) %reduce-scatter.8.cloned.1.call-update) | async-done | bytes 262160 | tf_op jit(solution)/shard_map/reduce_scatter | solution.py:123
  112.8 12.4 %fusion.61 = bf16[2048,256]{0,1:T(8,128)(2,1)} fusion(bf16[2,2048,4,512]{3,2,1,0:T(4,128)(2,1)} %bitcast.316, bf16[1,4,512,256]{2,3,1,0:T(8,128)(2,1)} %copy.50, bf16[1,4,512,256]{2,3,1,0:T(8,128)(2,1)S(1)} %bitcast.297), kind=kOutput, calls=%fused_computation.37 | convolution fusion | flops 4296540160 | bytes 19922944 | tf_op jit(solution)/shard_map/dot_general | solution.py:46
  125.7 26.2 %reduce-scatter.10.cloned.1.call-done = bf16[512,256]{0,1:T(8,128)(2,1)} async-done(((bf16[2048,256]{0,1:T(8,128)(2,1)}), bf16[512,256]{0,1:T(8,128)(2,1)}) %reduce-scatter.10.cloned.1.call-update) | async-done | bytes 262160 | tf_op jit(solution)/shard_map/reduce_scatter | solution.py:123
  165.1 12.4 %fusion.64 = bf16[2048,256]{0,1:T(8,128)(2,1)} fusion(bf16[2,2048,4,512]{3,2,1,0:T(4,128)(2,1)} %bitcast.314, bf16[1,4,512,256]{2,3,1,0:T(8,128)(2,1)} %copy.55, bf16[1,4,512,256]{2,3,1,0:T(8,128)(2,1)S(1)} %bitcast.267), kind=kOutput, calls=%fused_computation.38 | convolution fusion | flops 4296540160 | bytes 19922944 | tf_op jit(solution)/shard_map/dot_general | solution.py:46
  178.2 25.7 %reduce-scatter.12.cloned.1.call-done = bf16[512,256]{0,1:T(8,128)(2,1)} async-done(((bf16[2048,256]{0,1:T(8,128)(2,1)}), bf16[512,256]{0,1:T(8,128)(2,1)}) %reduce-scatter.12.cloned.1.call-update) | async-done | bytes 262160 | tf_op jit(solution)/shard_map/reduce_scatter | solution.py:123
  233.4 19.6 %fusion.73 = bf16[2048,256]{0,1:T(8,128)(2,1)} fusion(bf16[2,2048,8,512]{3,2,1,0:T(8,128)(2,1)} %bitcast.312, bf16[1,8,512,128]{2,3,1,0:T(8,128)(2,1)S(1)} %bitcast.296, bf16[1,8,512,128]{2,3,1,0:T(8,128)(2,1)S(1)} %neg.39, bf16[1,8,512,128]{2,3,1,0:T(8,128)(2,1)S(1)} %bitcast.269), kind=kOutput, calls=%fused_computation.41 | convolution fusion | flops 8607236096 | bytes 37748736 | tf_op jit(solution)/shard_map/dot_general | solution.py:46
  253.0 25.1 %reduce-scatter.14.cloned.1.call-done = bf16[512,256]{0,1:T(8,128)(2,1)} async-done(((bf16[2048,256]{0,1:T(8,128)(2,1)}), bf16[512,256]{0,1:T(8,128)(2,1)}) %reduce-scatter.14.cloned.1.call-update) | async-done | bytes 262160 | tf_op jit(solution)/shard_map/reduce_scatter | solution.py:123
  281.9 7.4 %collective-permute-done.18 = bf16[512,256]{0,1:T(8,128)(2,1)S(1)} collective-permute-done((bf16[512,256]{0,1:T(8,128)(2,1)}, bf16[512,256]{0,1:T(8,128)(2,1)S(1)}, u32[]{:S(2)}, u32[]{:S(2)}) %collective-permute-start.18) | collective-permute-done | bytes 262176 | tf_op jit(solution)/shard_map/ppermute | solution.py:17
  291.6 7.4 %collective-permute-done.20 = bf16[512,256]{0,1:T(8,128)(2,1)S(1)} collective-permute-done((bf16[512,256]{0,1:T(8,128)(2,1)S(1)}, bf16[512,256]{0,1:T(8,128)(2,1)S(1)}, u32[]{:S(2)}, u32[]{:S(2)}) %collective-permute-start.20) | collective-permute-done | bytes 262176 | tf_op jit(solution)/shard_map/ppermute | solution.py:17
  299.2 23.9 %fusion = f32[256,8,512,1]{2,0,3,1:T(8,128)} fusion(bf16[2,2048,8,512]{3,2,1,0:T(8,128)(2,1)} %bitcast.313, bf16[1,2048,256]{1,2,0:T(8,128)(2,1)S(1)} %maximum_bitcast_fusion.14, bf16[1,2048,256]{1,2,0:T(8,128)(2,1)S(1)} %bitcast.278), kind=kOutput, calls=%fused_computation | convolution fusion | flops 8594128896 | bytes 39845888 | tf_op jit(solution)/shard_map/dot_general | solution.py:55
  365.2 7.2 %collective-permute-done.27 = bf16[512,256]{0,1:T(8,128)(2,1)S(1)} collective-permute-done((bf16[512,256]{0,1:T(8,128)(2,1)S(1)}, bf16[512,256]{0,1:T(8,128)(2,1)S(1)}, u32[]{:S(2)}, u32[]{:S(2)}) %collective-permute-start.27) | collective-permute-done | bytes 262176 | tf_op jit(solution)/shard_map/ppermute | solution.py:17
  380.9 8.2 %fusion.6 = f32[256,4,512,1]{2,0,3,1:T(8,128)S(1)} fusion(bf16[2,2048,4,512]{3,2,1,0:T(4,128)(2,1)} %bitcast.315, bf16[1,2048,256]{1,2,0:T(8,128)(2,1)S(1)} %maximum_bitcast_fusion.15, bf16[1,2048,256]{1,2,0:T(8,128)(2,1)S(1)} %bitcast.276), kind=kOutput, calls=%fused_computation.6 | convolution fusion | flops 4299161600 | bytes 20971520 | tf_op jit(solution)/shard_map/dot_general | solution.py:55
  397.6 7.1 %collective-permute-done.31 = bf16[512,256]{0,1:T(8,128)(2,1)S(1)} collective-permute-done((bf16[512,256]{0,1:T(8,128)(2,1)S(1)}, bf16[512,256]{0,1:T(8,128)(2,1)S(1)}, u32[]{:S(2)}, u32[]{:S(2)}) %collective-permute-start.31) | collective-permute-done | bytes 262176 | tf_op jit(solution)/shard_map/ppermute | solution.py:34
  408.9 7.2 %collective-permute-done.32 = bf16[512,256]{0,1:T(8,128)(2,1)S(1)} collective-permute-done((bf16[512,256]{0,1:T(8,128)(2,1)S(1)}, bf16[512,256]{0,1:T(8,128)(2,1)S(1)}, u32[]{:S(2)}, u32[]{:S(2)}) %collective-permute-start.32) | collective-permute-done | bytes 262176 | tf_op jit(solution)/shard_map/ppermute | solution.py:17
  418.1 7.4 %collective-permute-done.34 = bf16[512,256]{0,1:T(8,128)(2,1)S(1)} collective-permute-done((bf16[512,256]{0,1:T(8,128)(2,1)S(1)}, bf16[512,256]{0,1:T(8,128)(2,1)S(1)}, u32[]{:S(2)}, u32[]{:S(2)}) %collective-permute-start.34) | collective-permute-done | bytes 262176 | tf_op jit(solution)/shard_map/ppermute | solution.py:17
  425.7 8.2 %fusion.4 = f32[256,4,512,1]{2,0,3,1:T(8,128)S(1)} fusion(bf16[2,2048,4,512]{3,2,1,0:T(4,128)(2,1)} %bitcast.317, bf16[1,2048,256]{1,2,0:T(8,128)(2,1)S(1)} %maximum_bitcast_fusion.16, bf16[1,2048,256]{1,2,0:T(8,128)(2,1)S(1)} %bitcast.271), kind=kOutput, calls=%fused_computation.4 | convolution fusion | flops 4299161600 | bytes 20971520 | tf_op jit(solution)/shard_map/dot_general | solution.py:55
  442.3 7.1 %collective-permute-done.36 = bf16[512,256]{0,1:T(8,128)(2,1)S(1)} collective-permute-done((bf16[512,256]{0,1:T(8,128)(2,1)S(1)}, bf16[512,256]{0,1:T(8,128)(2,1)S(1)}, u32[]{:S(2)}, u32[]{:S(2)}) %collective-permute-start.36) | collective-permute-done | bytes 262176 | tf_op jit(solution)/shard_map/ppermute | solution.py:34
  469.0 7.2 %collective-permute-done.39 = bf16[512,256]{0,1:T(8,128)(2,1)S(1)} collective-permute-done((bf16[512,256]{0,1:T(8,128)(2,1)S(1)}, bf16[512,256]{0,1:T(8,128)(2,1)S(1)}, u32[]{:S(2)}, u32[]{:S(2)}) %collective-permute-start.39) | collective-permute-done | bytes 262176 | tf_op jit(solution)/shard_map/ppermute | solution.py:17
  478.2 7.4 %collective-permute-done.41 = bf16[512,256]{0,1:T(8,128)(2,1)S(1)} collective-permute-done((bf16[512,256]{0,1:T(8,128)(2,1)S(1)}, bf16[512,256]{0,1:T(8,128)(2,1)S(1)}, u32[]{:S(2)}, u32[]{:S(2)}) %collective-permute-start.41) | collective-permute-done | bytes 262176 | tf_op jit(solution)/shard_map/ppermute | solution.py:17
  497.5 7.2 %collective-permute-done.43 = bf16[512,256]{0,1:T(8,128)(2,1)S(1)} collective-permute-done((bf16[512,256]{0,1:T(8,128)(2,1)S(1)}, bf16[512,256]{0,1:T(8,128)(2,1)S(1)}, u32[]{:S(2)}, u32[]{:S(2)}) %collective-permute-start.43) | collective-permute-done | bytes 262176 | tf_op jit(solution)/shard_map/ppermute | solution.py:17
  507.7 7.4 %collective-permute-done.45 = bf16[512,256]{0,1:T(8,128)(2,1)S(1)} collective-permute-done((bf16[512,256]{0,1:T(8,128)(2,1)S(1)}, bf16[512,256]{0,1:T(8,128)(2,1)S(1)}, u32[]{:S(2)}, u32[]{:S(2)}) %collective-permute-start.45) | collective-permute-done | bytes 262176 | tf_op jit(solution)/shard_map/ppermute | solution.py:17
  (322 shorter events, 213.5 us)
Async XLA Ops:
  7.2 45.3 %reduce-scatter.6.cloned.1.call-start = ((), (), s32[]{:S(2)}) async-start(), calls=%async_computation.5 | async-start | bytes 1310720 | tf_op jit(solution)/shard_map/reduce_scatter | solution.py:123
  22.4 67.3 %reduce-scatter.8.cloned.1.call-start = ((), (), s32[]{:S(2)}) async-start(), calls=%async_computation.6 | async-start | bytes 1310720 | tf_op jit(solution)/shard_map/reduce_scatter | solution.py:123
  63.7 88.2 %reduce-scatter.10.cloned.1.call-start = ((), (), s32[]{:S(2)}) async-start(), calls=%async_computation.7 | async-start | bytes 1310720 | tf_op jit(solution)/shard_map/reduce_scatter | solution.py:123
  64.0 28.6 %collective-permute-start.1 = (s32[4]{0:T(128)S(1)}, s32[4]{0:T(128)S(1)}, u32[]{:S(2)}, u32[]{:S(2)}) collective-permute-start(s32[4]{0:T(128)S(1)} %get-tuple-element.54), channel_id=1, source_target_pairs={{0,2},{2,0},{1,3},{3,1},{4,6},{6,4},{5,7},{7,5},{8,10},{10,8},{9,1... | collective-permute-start | bytes 56 | tf_op jit(solution)/shard_map/ppermute | solution.py:34
  125.3 78.6 %reduce-scatter.12.cloned.1.call-start = ((), (), s32[]{:S(2)}) async-start(), calls=%async_computation.8 | async-start | bytes 1310720 | tf_op jit(solution)/shard_map/reduce_scatter | solution.py:123
  177.6 100.5 %reduce-scatter.14.cloned.1.call-start = ((), (), s32[]{:S(2)}) async-start(), calls=%async_computation.9 | async-start | bytes 1310720 | tf_op jit(solution)/shard_map/reduce_scatter | solution.py:123
  278.1 11.2 %collective-permute-start.18 = (bf16[512,256]{0,1:T(8,128)(2,1)}, bf16[512,256]{0,1:T(8,128)(2,1)S(1)}, u32[]{:S(2)}, u32[]{:S(2)}) collective-permute-start(bf16[512,256]{0,1:T(8,128)(2,1)} %reduce-scatter.14.cloned.1.call-done), channel_id=1, source_target_pairs={{0,8},{8,16},{16,24},{24,0},{1,9},{9,17},{17,25},{25,1},{2,10},{10... | collective-permute-start | bytes 786440 | tf_op jit(solution)/shard_map/ppermute | solution.py:17
  278.1 13.5 %collective-permute-start.19 = (bf16[512,256]{0,1:T(8,128)(2,1)}, bf16[512,256]{0,1:T(8,128)(2,1)S(1)}, u32[]{:S(2)}, u32[]{:S(2)}) collective-permute-start(bf16[512,256]{0,1:T(8,128)(2,1)} %reduce-scatter.14.cloned.1.call-done), channel_id=1, source_target_pairs={{0,24},{8,0},{16,8},{24,16},{1,25},{9,1},{17,9},{25,17},{2,26},{10... | collective-permute-start | bytes 786440 | tf_op jit(solution)/shard_map/ppermute | solution.py:20
  289.3 9.7 %collective-permute-start.20 = (bf16[512,256]{0,1:T(8,128)(2,1)S(1)}, bf16[512,256]{0,1:T(8,128)(2,1)S(1)}, u32[]{:S(2)}, u32[]{:S(2)}) collective-permute-start(bf16[512,256]{0,1:T(8,128)(2,1)S(1)} %collective-permute-done.18), channel_id=1, source_target_pairs={{0,8},{8,16},{16,24},{24,0},{1,9},{9,17},{17,25},{25,1},{2,10},{10... | collective-permute-start | bytes 786440 | tf_op jit(solution)/shard_map/ppermute | solution.py:17
  325.8 10.4 %collective-permute-start.21 = (bf16[2,2,512,256]{2,3,0,1:T(8,128)(2,1)}, bf16[2,2,512,256]{2,3,0,1:T(8,128)(2,1)S(1)}, u32[]{:S(2)}, u32[]{:S(2)}) collective-permute-start(bf16[2,2,512,256]{2,3,0,1:T(8,128)(2,1)} %fusion.100), channel_id=1, source_target_pairs={{0,1},{1,0},{2,3},{3,2},{4,5},{5,4},{6,7},{7,6},{8,9},{9,8},{10,11... | collective-permute-start | bytes 3145736 | tf_op jit(solution)/shard_map/ppermute | solution.py:34
  361.3 11.0 %collective-permute-start.27 = (bf16[512,256]{0,1:T(8,128)(2,1)S(1)}, bf16[512,256]{0,1:T(8,128)(2,1)S(1)}, u32[]{:S(2)}, u32[]{:S(2)}) collective-permute-start(bf16[512,256]{0,1:T(8,128)(2,1)S(1)} %get-tuple-element.17), channel_id=1, source_target_pairs={{0,8},{8,16},{16,24},{24,0},{1,9},{9,17},{17,25},{25,1},{2,10},{10... | collective-permute-start | bytes 786440 | tf_op jit(solution)/shard_map/ppermute | solution.py:17
  361.4 13.0 %collective-permute-start.28 = (bf16[512,256]{0,1:T(8,128)(2,1)S(1)}, bf16[512,256]{0,1:T(8,128)(2,1)S(1)}, u32[]{:S(2)}, u32[]{:S(2)}) collective-permute-start(bf16[512,256]{0,1:T(8,128)(2,1)S(1)} %get-tuple-element.17), channel_id=1, source_target_pairs={{0,24},{8,0},{16,8},{24,16},{1,25},{9,1},{17,9},{25,17},{2,26},{10... | collective-permute-start | bytes 786440 | tf_op jit(solution)/shard_map/ppermute | solution.py:20
  405.0 11.0 %collective-permute-start.32 = (bf16[512,256]{0,1:T(8,128)(2,1)S(1)}, bf16[512,256]{0,1:T(8,128)(2,1)S(1)}, u32[]{:S(2)}, u32[]{:S(2)}) collective-permute-start(bf16[512,256]{0,1:T(8,128)(2,1)S(1)} %get-tuple-element.15), channel_id=1, source_target_pairs={{0,8},{8,16},{16,24},{24,0},{1,9},{9,17},{17,25},{25,1},{2,10},{10... | collective-permute-start | bytes 786440 | tf_op jit(solution)/shard_map/ppermute | solution.py:17
  405.1 13.0 %collective-permute-start.33 = (bf16[512,256]{0,1:T(8,128)(2,1)S(1)}, bf16[512,256]{0,1:T(8,128)(2,1)S(1)}, u32[]{:S(2)}, u32[]{:S(2)}) collective-permute-start(bf16[512,256]{0,1:T(8,128)(2,1)S(1)} %get-tuple-element.15), channel_id=1, source_target_pairs={{0,24},{8,0},{16,8},{24,16},{1,25},{9,1},{17,9},{25,17},{2,26},{10... | collective-permute-start | bytes 786440 | tf_op jit(solution)/shard_map/ppermute | solution.py:20
  416.0 9.5 %collective-permute-start.34 = (bf16[512,256]{0,1:T(8,128)(2,1)S(1)}, bf16[512,256]{0,1:T(8,128)(2,1)S(1)}, u32[]{:S(2)}, u32[]{:S(2)}) collective-permute-start(bf16[512,256]{0,1:T(8,128)(2,1)S(1)} %collective-permute-done.32), channel_id=1, source_target_pairs={{0,8},{8,16},{16,24},{24,0},{1,9},{9,17},{17,25},{25,1},{2,10},{10... | collective-permute-start | bytes 786440 | tf_op jit(solution)/shard_map/ppermute | solution.py:17
  440.2 9.2 %collective-permute-start.36 = (bf16[512,256]{0,1:T(8,128)(2,1)S(1)}, bf16[512,256]{0,1:T(8,128)(2,1)S(1)}, u32[]{:S(2)}, u32[]{:S(2)}) collective-permute-start(bf16[512,256]{0,1:T(8,128)(2,1)S(1)} %fusion.119), channel_id=1, source_target_pairs={{0,2},{2,0},{1,3},{3,1},{4,6},{6,4},{5,7},{7,5},{8,10},{10,8},{9,1... | collective-permute-start | bytes 786440 | tf_op jit(solution)/shard_map/ppermute | solution.py:34
  441.4 13.6 %collective-permute-start.38 = (bf16[512,256]{0,1:T(8,128)(2,1)}, bf16[512,256]{0,1:T(8,128)(2,1)S(1)}, u32[]{:S(2)}, u32[]{:S(2)}) collective-permute-start(bf16[512,256]{0,1:T(8,128)(2,1)} %copy-done.10), channel_id=1, source_target_pairs={{0,2},{2,0},{1,3},{3,1},{4,6},{6,4},{5,7},{7,5},{8,10},{10,8},{9,1... | collective-permute-start | bytes 786440 | tf_op jit(solution)/shard_map/ppermute | solution.py:34
  449.5 10.2 %collective-permute-start.37 = (bf16[512,256]{0,1:T(8,128)(2,1)S(1)}, bf16[512,256]{0,1:T(8,128)(2,1)S(1)}, u32[]{:S(2)}, u32[]{:S(2)}) collective-permute-start(bf16[512,256]{0,1:T(8,128)(2,1)S(1)} %get-tuple-element.12), channel_id=1, source_target_pairs={{0,2},{2,0},{1,3},{3,1},{4,6},{6,4},{5,7},{7,5},{8,10},{10,8},{9,1... | collective-permute-start | bytes 786440 | tf_op jit(solution)/shard_map/ppermute | solution.py:34
  465.1 11.0 %collective-permute-start.39 = (bf16[512,256]{0,1:T(8,128)(2,1)S(1)}, bf16[512,256]{0,1:T(8,128)(2,1)S(1)}, u32[]{:S(2)}, u32[]{:S(2)}) collective-permute-start(bf16[512,256]{0,1:T(8,128)(2,1)S(1)} %get-tuple-element.11), channel_id=1, source_target_pairs={{0,8},{8,16},{16,24},{24,0},{1,9},{9,17},{17,25},{25,1},{2,10},{10... | collective-permute-start | bytes 786440 | tf_op jit(solution)/shard_map/ppermute | solution.py:17
  465.1 13.0 %collective-permute-start.40 = (bf16[512,256]{0,1:T(8,128)(2,1)S(1)}, bf16[512,256]{0,1:T(8,128)(2,1)S(1)}, u32[]{:S(2)}, u32[]{:S(2)}) collective-permute-start(bf16[512,256]{0,1:T(8,128)(2,1)S(1)} %get-tuple-element.11), channel_id=1, source_target_pairs={{0,24},{8,0},{16,8},{24,16},{1,25},{9,1},{17,9},{25,17},{2,26},{10... | collective-permute-start | bytes 786440 | tf_op jit(solution)/shard_map/ppermute | solution.py:20
  476.1 9.5 %collective-permute-start.41 = (bf16[512,256]{0,1:T(8,128)(2,1)S(1)}, bf16[512,256]{0,1:T(8,128)(2,1)S(1)}, u32[]{:S(2)}, u32[]{:S(2)}) collective-permute-start(bf16[512,256]{0,1:T(8,128)(2,1)S(1)} %collective-permute-done.39), channel_id=1, source_target_pairs={{0,8},{8,16},{16,24},{24,0},{1,9},{9,17},{17,25},{25,1},{2,10},{10... | collective-permute-start | bytes 786440 | tf_op jit(solution)/shard_map/ppermute | solution.py:17
  493.6 11.1 %collective-permute-start.43 = (bf16[512,256]{0,1:T(8,128)(2,1)S(1)}, bf16[512,256]{0,1:T(8,128)(2,1)S(1)}, u32[]{:S(2)}, u32[]{:S(2)}) collective-permute-start(bf16[512,256]{0,1:T(8,128)(2,1)S(1)} %get-tuple-element.9), channel_id=1, source_target_pairs={{0,8},{8,16},{16,24},{24,0},{1,9},{9,17},{17,25},{25,1},{2,10},{10... | collective-permute-start | bytes 786440 | tf_op jit(solution)/shard_map/ppermute | solution.py:17
  493.7 14.0 %collective-permute-start.44 = (bf16[512,256]{0,1:T(8,128)(2,1)S(1)}, bf16[512,256]{0,1:T(8,128)(2,1)S(1)}, u32[]{:S(2)}, u32[]{:S(2)}) collective-permute-start(bf16[512,256]{0,1:T(8,128)(2,1)S(1)} %get-tuple-element.9), channel_id=1, source_target_pairs={{0,24},{8,0},{16,8},{24,16},{1,25},{9,1},{17,9},{25,17},{2,26},{10... | collective-permute-start | bytes 786440 | tf_op jit(solution)/shard_map/ppermute | solution.py:20
  504.7 10.4 %collective-permute-start.45 = (bf16[512,256]{0,1:T(8,128)(2,1)S(1)}, bf16[512,256]{0,1:T(8,128)(2,1)S(1)}, u32[]{:S(2)}, u32[]{:S(2)}) collective-permute-start(bf16[512,256]{0,1:T(8,128)(2,1)S(1)} %collective-permute-done.43), channel_id=1, source_target_pairs={{0,8},{8,16},{16,24},{24,0},{1,9},{9,17},{17,25},{25,1},{2,10},{10... | collective-permute-start | bytes 786440 | tf_op jit(solution)/shard_map/ppermute | solution.py:17
  (49 other events, 303.6 us)
Sparse Core Ops, SparseCore 0:
  22.5 29.8 reduce-scatter.5
  63.8 25.7 reduce-scatter.7
  125.4 26.4 reduce-scatter.9
  177.7 26.1 reduce-scatter.11
  253.1 24.9 reduce-scatter.13
